TPU v7x, 32 devices: a whole 2x2x4 slice. The times are simulated.
32 devices in a mesh: dp: 8 (over z, y), group: 4 (over x, core).
Axes of the slice: x: 2, y: 2, z: 4, core: 2. Of those that a mesh axis runs over, the one named last changes fastest.
Arguments:
- waveform: bfloat16 [128, 2560], P(('dp', 'group')), may hold values from -6 to 6
- lengths: int32 [128], P(('dp', 'group')), may hold values from 1280 to 2560
- packing: int32 [128], P(('dp', 'group')), may hold values from 0 to 15, as said below
- first_weight: bfloat16 [512, 10], P('dp'), may hold values from -2 to 2
- norm_gain: float32 [512], replicated, may hold values from 0.25 to 1.75
- norm_bias: float32 [512], replicated, may hold values from -3 to 3
- conv_weight: bfloat16 [512, 1536], P('dp'), may hold values from -0.15625 to 0.15625
- grad_features: bfloat16 [128, 255, 512], P(('dp', 'group')), may hold values from -0.25 to 0.25
Outputs:
- features: bfloat16 [128, 255, 512], P(('dp', 'group'))
- grad_conv: float32 [512, 1536], P('dp')
- grad_first: float32 [512, 10], P('dp')
- grad_gain: float32 [512], replicated
- grad_bias: float32 [512], replicated
Inputs may be any that keep to these rules, and one draw needn't show every extreme that they name: `packing`: within each index of dp the 16 rows form a permutation of the positions of that index's block; position p lies on the device of group index p // 4 of the same dp index. Each device sends an even number of its rows to each device of its group, at most 2 to one device, and exactly 2 to some.
All inputs are finite; a program needn't handle non-finite values.
Results may differ from a plain program's by a relative error of at most 0.0057.
Values may be sent and summed in bfloat16 or wider, within the bound.
A program may use at most 64 MiB of HBM per device.

v0:
```python
import jax
import jax.numpy as jnp
from jax import lax
from jax.sharding import PartitionSpec as P


def gelu_slope(values):
    return (
        0.5 * (1.0 + lax.erf(values * 0.7071067811865476))
        + values * jnp.exp(-0.5 * values * values) * 0.3989422804014327
    )


def tap_matrix(hidden, frames_second):
    row_count, frames_first, channels = hidden.shape
    zero_frame = jnp.zeros((row_count, 1, channels), hidden.dtype)
    paired = jnp.concatenate([hidden, zero_frame], axis=1).reshape(
        row_count, frames_second + 1, 2, channels
    )
    even_half = paired[:, :, 0]
    odd_half = paired[:, :, 1]
    stacked = jnp.concatenate(
        [even_half[:, :frames_second], odd_half[:, :frames_second], even_half[:, 1:]], axis=2
    )
    return stacked.reshape(row_count * frames_second, 3 * channels)


def spread_back(back_taps, row_count, frames_second, frames_first):
    first_tap = back_taps[0].reshape(row_count, frames_second, -1)
    middle_tap = back_taps[1].reshape(row_count, frames_second, -1)
    last_tap = back_taps[2].reshape(row_count, frames_second, -1)
    channels = first_tap.shape[2]
    zero_frame = jnp.zeros((row_count, 1, channels), jnp.float32)
    even_half = jnp.concatenate([first_tap, zero_frame], axis=1) + jnp.concatenate(
        [zero_frame, last_tap], axis=1
    )
    odd_half = jnp.concatenate([middle_tap, zero_frame], axis=1)
    joined = jnp.stack([even_half, odd_half], axis=2).reshape(
        row_count, 2 * frames_second + 2, channels
    )
    return joined[:, :frames_first]


def local(
    waveform, lengths, packing, first_weight, norm_gain, norm_bias, conv_weight, grad_features
):
    row_count, capacity = waveform.shape
    channels = norm_gain.shape[0]
    frames_first = capacity // 5 - 1
    frames_second = (capacity // 5 - 2) // 2
    groups = lax.axis_size("group")
    own_group = lax.axis_index("group")
    group_rows = groups * row_count
    all_pack, all_lengths = (
        lax.all_gather(packing, "group", axis=0, tiled=True),
        lax.all_gather(lengths, "group", axis=0, tiled=True),
    )
    target = all_pack // row_count
    slot_index = all_pack % row_count
    positions = jnp.arange(group_rows)
    source = positions // row_count
    same_source = source[:, None] == source[None, :]
    same_target = target[:, None] == target[None, :]
    before = positions[:, None] > positions[None, :]
    rank_among = jnp.sum((same_source & same_target & before).astype(jnp.int32), axis=1)
    arriving = target == own_group
    slot_ids = jnp.arange(row_count)
    choose_slot = (slot_index[None, :] == slot_ids[:, None]) & arriving[None, :]
    local_lengths = jnp.sum(jnp.where(choose_slot, all_lengths[None, :], 0), axis=1)
    per_peer = 2 * ((row_count + 2 * groups - 1) // (2 * groups))
    lane_ids = jnp.arange(per_peer)
    own_target = lax.dynamic_slice_in_dim(target, own_group * row_count, row_count)
    own_rank = lax.dynamic_slice_in_dim(rank_among, own_group * row_count, row_count)
    outgoing = (
        (own_target[None, None, :] == jnp.arange(groups)[:, None, None])
        & (own_rank[None, None, :] == lane_ids[None, :, None])
    ).astype(jnp.bfloat16)
    send_rows = jnp.einsum(
        "gkr,rs->gks", outgoing, waveform, preferred_element_type=jnp.float32
    ).astype(jnp.bfloat16)
    received = lax.all_to_all(send_rows, "group", split_axis=0, concat_axis=0, tiled=True)
    pick_slots = (
        choose_slot[:, :, None] & (rank_among[None, :, None] == lane_ids[None, None, :])
    ).astype(jnp.float32)
    pick_slots = jnp.sum(pick_slots.reshape(row_count, groups, row_count, per_peer), axis=2).astype(
        jnp.bfloat16
    )
    wave_rows = jnp.einsum(
        "lsk,skn->ln", pick_slots, received, preferred_element_type=jnp.float32
    ).astype(jnp.bfloat16)
    first_whole = lax.all_gather(first_weight, "dp", axis=0, tiled=True)
    in_length = jnp.arange(capacity)[None, :] < local_lengths[:, None]
    masked = jnp.where(in_length, wave_rows, jnp.zeros_like(wave_rows))
    blocks = masked.reshape(row_count, capacity // 5, 5)
    taps_first = jnp.concatenate([blocks[:, :-1], blocks[:, 1:]], axis=2).reshape(
        row_count * frames_first, 10
    )
    conv_first = lax.dot_general(
        taps_first, first_whole, (((1,), (1,)), ((), ())), preferred_element_type=jnp.float32
    )
    conv_first = conv_first.reshape(row_count, frames_first, channels)
    count_first = (local_lengths - 10) // 5 + 1
    count_second = (count_first - 3) // 2 + 1
    valid_first = (jnp.arange(frames_first)[None, :] < count_first[:, None]).astype(jnp.float32)[
        :, :, None
    ]
    valid_second = (jnp.arange(frames_second)[None, :] < count_second[:, None]).astype(jnp.float32)[
        :, :, None
    ]
    count_float = count_first.astype(jnp.float32)[:, None, None]
    row_mean = jnp.sum(conv_first * valid_first, axis=1, keepdims=True) / count_float
    centred = (conv_first - row_mean) * valid_first
    row_var = jnp.sum(centred * centred, axis=1, keepdims=True) / count_float
    inv_scale = lax.rsqrt(row_var + 1e-05)
    normed = (conv_first - row_mean) * inv_scale
    shifted = normed * norm_gain + norm_bias
    hidden = (jax.nn.gelu(shifted, approximate=False) * valid_first).astype(jnp.bfloat16)
    taps_second = tap_matrix(hidden, frames_second)
    conv_whole = lax.all_gather(conv_weight, "dp", axis=0, tiled=True)
    conv_second = lax.dot_general(
        taps_second, conv_whole, (((1,), (1,)), ((), ())), preferred_element_type=jnp.float32
    )
    conv_second = conv_second.reshape(row_count, frames_second, channels)
    features = (jax.nn.gelu(conv_second, approximate=False) * valid_second).astype(jnp.bfloat16)
    delta_second = (
        grad_features.astype(jnp.float32) * valid_second * gelu_slope(conv_second)
    ).astype(jnp.bfloat16)
    delta_flat = delta_second.reshape(row_count * frames_second, channels)
    back_taps = tuple(
        (
            jnp.dot(
                delta_flat,
                conv_whole[:, tap_index * channels : (tap_index + 1) * channels],
                preferred_element_type=jnp.float32,
            )
            for tap_index in range(3)
        )
    )
    share = lax.psum_scatter(
        lax.dot_general(
            delta_flat, taps_second, (((0,), (0,)), ((), ())), preferred_element_type=jnp.float32
        ),
        "dp",
        scatter_dimension=0,
        tiled=True,
    )
    grad_conv = lax.psum(share, "group")
    delta_hidden = spread_back(back_taps, row_count, frames_second, frames_first)
    delta_norm = delta_hidden * valid_first * gelu_slope(shifted)
    gain_term = jnp.sum(delta_norm * normed, axis=(0, 1))
    bias_term = jnp.sum(delta_norm, axis=(0, 1))
    scaled = delta_norm * norm_gain
    mean_grad = jnp.sum(scaled, axis=1, keepdims=True) / count_float
    mean_cross = jnp.sum(scaled * normed, axis=1, keepdims=True) / count_float
    delta_first = ((scaled - mean_grad - normed * mean_cross) * inv_scale * valid_first).astype(
        jnp.bfloat16
    )
    first_term = lax.dot_general(
        delta_first.reshape(row_count * frames_first, channels),
        taps_first,
        (((0,), (0,)), ((), ())),
        preferred_element_type=jnp.float32,
    )
    stacked = jnp.concatenate([first_term, gain_term[:, None], bias_term[:, None]], axis=1)
    summed = lax.psum(stacked, ("dp", "group"))
    shard_rows = channels // lax.axis_size("dp")
    grad_first = lax.dynamic_slice_in_dim(
        summed[:, :10], lax.axis_index("dp") * shard_rows, shard_rows, 0
    )
    return (features, grad_conv, grad_first, summed[:, 10], summed[:, 11])


def solution(mesh):
    return jax.shard_map(
        local,
        mesh=mesh,
        in_specs=(
            P(("dp", "group"), None),
            P(("dp", "group")),
            P(("dp", "group")),
            P("dp", None),
            P(),
            P(),
            P("dp", None),
            P(("dp", "group"), None, None),
        ),
        out_specs=(P(("dp", "group"), None, None), P("dp", None), P("dp", None), P(), P()),
        check_vma=False,
    )
```

profile of v0, /device:TPU:0, one launch (start us, length us, event | category | flops | bytes accessed | tf_op | source)
XLA Modules:
  0.0 210.4 jit_solution(2185405149943320980)
XLA Ops:
  7.2 0.7 all-gather.3.cloned.1.call-update
  7.9 1.2 dynamic-slice
  9.8 0.9 dynamic-update-slice
  10.7 0.8 dynamic-update-slice.1
  11.5 6.4 %all-reduce.6 = (s32[16]{0:T(128)S(1)}, s32[16]{0:T(128)S(1)}) all-reduce(s32[16]{0:T(128)S(1)} %dynamic-update-slice, s32[16]{0:T(128)S(1)} %dynamic-update-slice.1), channel_id=1, replica_groups=mesh['dp'=8,'group'=4] {'group'}, use_global_device_ids=true, to_apply=%add.4 | all-reduce | flops 32 | bytes 256
  19.1 3.3 %all-to-all-start = ((bf16[4,2,2560]{2,1,0:T(2,128)(2,1)}), bf16[4,2,2560]{2,1,0:T(2,128)(2,1)S(1)}, u32[]{:S(2)}, u32[]{:S(2)}) async-start(bf16[4,2,2560]{2,1,0:T(2,128)(2,1)} %copy.42), calls=%async_computation | async-start | bytes 81920 | tf_op jit(solution)/shard_map/all_to_all | solution.py:81
  23.2 31.5 %all-gather = bf16[8,64,10]{1,2,0:T(8,128)(2,1)S(1)} all-gather(bf16[1,64,10]{1,2,0:T(8,128)(2,1)} %bitcast.60), channel_id=1, replica_groups=mesh['dp'=8,'group'=4] {'dp'}, dimensions={0}, use_global_device_ids=true | all-gather | bytes 11520 | tf_op jit(solution)/shard_map/all_gather | solution.py:91
  55.1 1.0 reshape.327
  56.8 1.0 multiply_reduce_fusion.3
  57.9 0.7 multiply_reduce_fusion.2
  58.7 10.2 %fusion.3 = bf16[4,511,512]{2,1,0:T(8,128)(2,1)S(1)} fusion(f32[4,511,512]{2,1,0:T(8,128)S(1)} %get-tuple-element.51, f32[512]{0:T(512)S(1)} %copy-done.5, f32[512]{0:T(512)S(1)} %copy-done.6, f32[4,512]{1,0:T(4,128)S(1)} %add_rsqrt_fusion, f32[4,512]{1,0:T(4,128)S(1)} %broadcast_divide_fusion.2, f32[4,511]{1,0:T(4,128)S(1)} %fusion.46), kind=kLoop, calls=%fused_computation.5 | loop fusion | flops 73256960 | bytes 6307824 | tf_op jit(solution)/shard_map/convert_element_type | solution.py:117
  68.9 1.5 concatenate.22
  70.4 2.7 %reshape.328 = bf16[4,256,2,512]{3,2,1,0:T(2,128)(2,1)S(1)} reshape(bf16[4,512,512]{2,1,0:T(8,128)(2,1)} %concatenate.22) | data formatting | bytes 4194304 | tf_op jit(solution)/shard_map/reshape | solution.py:17
  73.2 3.0 %fusion.59 = (bf16[4,256,1,512]{3,2,1,0:T(2,128)(2,1)S(1)}, bf16[4,256,1,512]{3,2,1,0:T(2,128)(2,1)S(1)}) fusion(bf16[4,256,2,512]{3,2,1,0:T(2,128)(2,1)S(1)} %reshape.328), kind=kLoop, calls=%fused_computation.134 | loop fusion | bytes 4194304 | tf_op jit(solution)/shard_map/slice | solution.py:21
  76.7 1.3 fusion.60
  78.1 10.2 %fusion.27 = (bf16[4,255,512]{2,1,0:T(8,128)(2,1)S(1)}, bf16[4,255,512]{2,1,0:T(8,128)(2,1)}) fusion(bf16[4,255,512]{2,0,1:T(4,128)(2,1)} %param.15, f32[4,255]{1,0:T(4,128)S(1)} %fusion.47, bf16[512,1536]{1,0:T(8,128)(2,1)} %all-gather.3.cloned.1.call-done, bf16[4,255,512]{2,1,0:T(8,128)(2,1)} %get-tuple-element.41, bf16[4,255,512]{2,1,0:T(8,128)(2,1)S(1)} %bitcast.55, ...), kind=kOutput, calls=%fused_computation.53 | convolution fusion | flops 1654456320 | bytes 7843824 | tf_op jit(solution)/shard_map/dot_general | solution.py:120
  88.3 3.5 %convolution_bitcast_fusion.1 = f32[512,1536]{1,0:T(8,128)} fusion(bf16[4,255,512]{2,1,0:T(8,128)(2,1)S(1)} %get-tuple-element.36, bf16[4,255,512]{2,1,0:T(8,128)(2,1)S(1)} %copy-done.4, bf16[4,255,512]{2,1,0:T(8,128)(2,1)S(1)} %bitcast.56, bf16[4,255,512]{2,1,0:T(8,128)(2,1)S(1)} %get-tuple-element.40), kind=kOutput, calls=%fused_computation.40 | convolution fusion | flops 1613721600 | bytes 7323648 | tf_op jit(solution)/shard_map/dot_general | solution.py:140
  92.0 3.1 %copy.53 = bf16[4,255,512]{2,0,1:T(4,128)(2,1)} copy(bf16[4,255,512]{2,1,0:T(8,128)(2,1)} %get-tuple-element.37) | data formatting | bytes 2088960
  95.2 0.7 fusion.39
  95.9 0.7 fusion.40
  96.6 0.7 fusion.41
  97.3 1.0 pad_bitcast_fusion
  98.3 0.7 pad_maximum_fusion
  99.0 5.2 %copy.52 = f32[4,256,2,512]{3,2,1,0:T(2,128)} copy(f32[4,256,2,512]{3,1,0,2:T(8,128)S(1)} %pad_maximum_fusion) | data formatting | bytes 8388608 | tf_op jit(solution)/shard_map/stack | solution.py:38
  104.2 6.1 %reshape.329 = f32[4,512,512]{2,1,0:T(8,128)} reshape(f32[4,256,2,512]{3,2,1,0:T(2,128)} %copy.52) | data formatting | bytes 8388608 | tf_op jit(solution)/shard_map/reshape | solution.py:38
  110.3 6.1 %multiply_reduce_fusion.1 = (f32[4,512]{1,0:T(4,128)S(1)}, f32[512]{0:T(512)S(1)}, f32[4,512]{1,0:T(4,128)S(1)}, f32[512]{0:T(512)S(1)}, f32[4,511,512]{2,1,0:T(8,128)S(1)}) fusion(f32[4,511,512]{2,1,0:T(8,128)} %copy-done.1, f32[512]{0:T(512)S(1)} %copy-done.6, f32[4,512]{1,0:T(4,128)S(1)} %add_rsqrt_fusion, f32[4,512]{1,0:T(4,128)S(1)} %broadcast_divide_fusion.2, ...), kind=kLoop, calls=%fused_computation.15 | loop fusion | flops 21971968 | bytes 12607472 | tf_op jit(solution)/shard_map/reduce_sum | solution.py:154
  116.4 1.3 fusion.38
  117.8 40.1 %psum.15 = f32[512,12]{0,1:T(8,128)S(1)} all-reduce(f32[512,12]{0,1:T(8,128)S(1)} %pad_maximum_fusion.7), channel_id=1, replica_groups=mesh['dp'=8,'group'=4] {'dp','group'}, use_global_device_ids=true, to_apply=%region_11.12 | all-reduce | flops 6144 | bytes 49152 | tf_op jit(solution)/shard_map/psum | solution.py:165
  157.9 0.7 constant_dynamic-slice_fusion
  158.6 9.3 %reduce-scatter.2.cloned.1.call-done = f32[64,1536]{1,0:T(8,128)} async-done(((f32[512,1536]{1,0:T(8,128)}), f32[64,1536]{1,0:T(8,128)}) %reduce-scatter.2.cloned.1.call-update) | async-done | bytes 393232 | tf_op jit(solution)/shard_map/reduce_scatter | solution.py:139
  168.5 33.6 %all-reduce.9.cloned.1.call-done = f32[64,1536]{1,0:T(8,128)} async-done(((f32[64,1536]{1,0:T(8,128)}), f32[64,1536]{1,0:T(8,128)}) %all-reduce.9.cloned.1.call-update) | async-done | bytes 393232 | tf_op jit(solution)/shard_map/psum | solution.py:147
  202.1 1.8 copy.72
  (58 shorter events, 4.7 us)
Async XLA Ops:
  7.2 11.1 %copy-start = (bf16[4,2560]{1,0:T(4,128)(2,1)S(1)}, bf16[4,2560]{1,0:T(4,128)(2,1)}, u32[]{:S(2)}) copy-start(bf16[4,2560]{1,0:T(4,128)(2,1)} %param.8) | copy-start | bytes 61444
  7.2 70.9 %all-gather.3.cloned.1.call-start = ((), (), s32[]{:S(2)}) async-start(), calls=%async_computation.2 | async-start | bytes 1769472 | tf_op jit(solution)/shard_map/all_gather | solution.py:119
  19.1 35.8 %all-to-all-start = ((bf16[4,2,2560]{2,1,0:T(2,128)(2,1)}), bf16[4,2,2560]{2,1,0:T(2,128)(2,1)S(1)}, u32[]{:S(2)}, u32[]{:S(2)}) async-start(bf16[4,2,2560]{2,1,0:T(2,128)(2,1)} %copy.42), calls=%async_computation | async-start | bytes 81920 | tf_op jit(solution)/shard_map/all_to_all | solution.py:81
  22.4 145.6 %reduce-scatter.2.cloned.1.call-start = ((), (), s32[]{:S(2)}) async-start(), calls=%async_computation.3 | async-start | bytes 3538944 | tf_op jit(solution)/shard_map/reduce_scatter | solution.py:139
  56.7 1.9 copy-start.5
  56.8 1.9 copy-start.6
  57.8 11.1 %copy-start.1 = (f32[4,511,512]{2,1,0:T(8,128)}, f32[4,511,512]{2,1,0:T(8,128)S(1)}, u32[]{:S(2)}) copy-start(f32[4,511,512]{2,1,0:T(8,128)S(1)} %get-tuple-element.51) | copy-start | bytes 12558340
  78.1 10.2 %copy-start.4 = (bf16[4,255,512]{2,1,0:T(8,128)(2,1)S(1)}, bf16[4,255,512]{2,1,0:T(8,128)(2,1)}, u32[]{:S(2)}) copy-start(bf16[4,255,512]{2,1,0:T(8,128)(2,1)} %get-tuple-element.41) | copy-start | bytes 3133444
  91.8 3.4 %copy-start.3 = (bf16[512,1536]{1,0:T(8,128)(2,1)S(1)}, bf16[512,1536]{1,0:T(8,128)(2,1)}, u32[]{:S(2)}) copy-start(bf16[512,1536]{1,0:T(8,128)(2,1)} %all-gather.3.cloned.1.call-done) | copy-start | bytes 4718596
  91.8 110.3 %all-reduce.9.cloned.1.call-start = ((), (), s32[]{:S(2)}) async-start(), calls=%async_computation.4 | async-start | bytes 786432 | tf_op jit(solution)/shard_map/psum | solution.py:147
  110.3 6.1 %copy-start.2 = (f32[4,511,512]{2,1,0:T(8,128)S(1)}, f32[4,511,512]{2,1,0:T(8,128)}, u32[]{:S(2)}) copy-start(f32[4,511,512]{2,1,0:T(8,128)} %copy-done.1) | copy-start | bytes 12558340
Sparse Core Ops, SparseCore 0:
  10.2 47.2 all-gather.2
  91.9 75.9 reduce-scatter.1
  170.3 31.7 all-reduce.8
where the time goes:
time: 211 us; the launch traced here: 210 us
  blocking collectives  78 us (37%)
  waiting for transfers between devices  43.6 us (21%)
  local copies, waits for them, and re-layouts  32.4 us (15%)
  other arithmetic  19.6 us (9%)
  matrix products  18.5 us (9%)
  between operations  14.7 us (7%)
  starting transfers between devices  3.57 us (2%)
    psum x1, blocking collectives, local(): summed = lax.psum(stacked, ('dp', 'group'))  40.1 us
    psum x1, waiting for transfers between devices, local(): grad_conv = lax.psum(share, 'group')  33.6 us
    all_gather x1, blocking collectives, local(): first_whole = lax.all_gather(first_weight, 'dp', axis=0, tiled=True)  31.5 us
    convert_element_type x1, other arithmetic, local(): (jax.nn.gelu(shifted, approximate=False) * valid_first).astype(jnp.bfloat16)  10.2 us
    dot_general x1, matrix products, local(): lax.dot_general(taps_second, conv_whole, (((1,), (1,)), ((), ())), prefer...  10.2 us
    reduce_scatter x1, waiting for transfers between devices, local(): lax.psum_scatter(lax.dot_general(delta_flat, taps_second, (((0,), (0,)),...  9.35 us
    unnamed x26, local copies, waits for them, and re-layouts  9.01 us
    unnamed x1, blocking collectives  6.38 us
  transfers between devices with their start and end apart: 4, of which 2 were waited for; matrix products, arithmetic and copies ran while one was open for 26% of the time, Pallas kernels for 0%

commit v1 on v0

--- a/solution.py
+++ b/solution.py
@@ -144,7 +144,7 @@
         scatter_dimension=0,
         tiled=True,
     )
-    grad_conv = lax.psum(share, "group")
+    grad_conv = jnp.sum(lax.all_gather(share, "group"), axis=0)
     delta_hidden = spread_back(back_taps, row_count, frames_second, frames_first)
     delta_norm = delta_hidden * valid_first * gelu_slope(shifted)
     gain_term = jnp.sum(delta_norm * normed, axis=(0, 1))

time: 211 us -> 239 us (1.13)
  waiting for transfers between devices: 43.6 us -> 69 us
  other arithmetic: 19.6 us -> 24.4 us
    reduce_scatter x1, waiting for transfers between devices: 9.35 us -> 68.2 us  [local(): lax.psum_scatter(lax.dot_general(delta_flat, taps_second, (((0,), (0,)),...]
    psum x1 -> x0, waiting for transfers between devices: 33.6 us -> none  [local(): grad_conv = lax.psum(share, 'group')]
    another operation x2, other arithmetic: 1.71 us -> 4.3 us  [spread_back(): jnp.stack([even_half, odd_half], axis=2)]
    unnamed x26 -> x25, local copies, waits for them, and re-layouts: 9.01 us -> 7.25 us
  transfers between devices with their start and end apart: 4 -> 4, of which waited for: 2 -> 1; matrix products, arithmetic and copies ran while one was open for 26% -> 24% of each run, Pallas kernels for 0% -> 0%
where the time goes in v1:
time: 239 us
  blocking collectives  77.8 us (33%)
  waiting for transfers between devices  69 us (29%)
  local copies, waits for them, and re-layouts  30.7 us (13%)
  other arithmetic  24.4 us (10%)
  matrix products  18.5 us (8%)
  between operations  14.7 us (6%)
  starting transfers between devices  3.57 us (1%)
    reduce_scatter x1, waiting for transfers between devices, local(): lax.psum_scatter(lax.dot_general(delta_flat, taps_second, (((0,), (0,)),...  68.2 us
    psum x1, blocking collectives, local(): summed = lax.psum(stacked, ('dp', 'group'))  39.9 us
    all_gather x1, blocking collectives, local(): first_whole = lax.all_gather(first_weight, 'dp', axis=0, tiled=True)  31.5 us
    convert_element_type x1, other arithmetic, local(): (jax.nn.gelu(shifted, approximate=False) * valid_first).astype(jnp.bfloat16)  10.2 us
    dot_general x1, matrix products, local(): lax.dot_general(taps_second, conv_whole, (((1,), (1,)), ((), ())), prefer...  10.2 us
    unnamed x25, local copies, waits for them, and re-layouts  7.25 us
    unnamed x1, blocking collectives  6.38 us
    reshape x1, local copies, waits for them, and re-layouts, spread_back(): jnp.stack([even_half, odd_half], axis=2)  6.07 us
  transfers between devices with their start and end apart: 4, of which 1 were waited for; matrix products, arithmetic and copies ran while one was open for 24% of the time, Pallas kernels for 0%

profile of v1, /device:TPU:0, one launch (start us, length us, event | category | flops | bytes accessed | tf_op | source)
XLA Modules:
  0.0 238.5 jit_solution(15657518686597699921)
XLA Ops:
  7.2 0.7 all-gather.5.cloned.1.call-update
  7.9 1.2 dynamic-slice
  9.8 0.9 dynamic-update-slice
  10.7 0.8 dynamic-update-slice.1
  11.5 6.4 %all-reduce.6 = (s32[16]{0:T(128)S(1)}, s32[16]{0:T(128)S(1)}) all-reduce(s32[16]{0:T(128)S(1)} %dynamic-update-slice, s32[16]{0:T(128)S(1)} %dynamic-update-slice.1), channel_id=1, replica_groups=mesh['dp'=8,'group'=4] {'group'}, use_global_device_ids=true, to_apply=%add.4 | all-reduce | flops 32 | bytes 256
  18.4 0.6 copy.42
  19.1 3.3 %all-to-all-start = ((bf16[4,2,2560]{2,1,0:T(2,128)(2,1)}), bf16[4,2,2560]{2,1,0:T(2,128)(2,1)S(1)}, u32[]{:S(2)}, u32[]{:S(2)}) async-start(bf16[4,2,2560]{2,1,0:T(2,128)(2,1)} %copy.42), calls=%async_computation | async-start | bytes 81920 | tf_op jit(solution)/shard_map/all_to_all | solution.py:81
  23.2 31.5 %all-gather.1 = bf16[8,64,10]{1,2,0:T(8,128)(2,1)S(1)} all-gather(bf16[1,64,10]{1,2,0:T(8,128)(2,1)} %bitcast.62), channel_id=1, replica_groups=mesh['dp'=8,'group'=4] {'dp'}, dimensions={0}, use_global_device_ids=true | all-gather | bytes 11520 | tf_op jit(solution)/shard_map/all_gather | solution.py:91
  55.1 1.0 reshape.327
  56.8 1.0 multiply_reduce_fusion.3
  57.9 0.7 multiply_reduce_fusion.2
  58.7 10.2 %fusion.3 = bf16[4,511,512]{2,1,0:T(8,128)(2,1)S(1)} fusion(f32[4,511,512]{2,1,0:T(8,128)S(1)} %get-tuple-element.51, f32[512]{0:T(512)S(1)} %copy-done.5, f32[512]{0:T(512)S(1)} %copy-done.6, f32[4,512]{1,0:T(4,128)S(1)} %add_rsqrt_fusion, f32[4,512]{1,0:T(4,128)S(1)} %broadcast_divide_fusion.2, f32[4,511]{1,0:T(4,128)S(1)} %fusion.46), kind=kLoop, calls=%fused_computation.5 | loop fusion | flops 73256960 | bytes 6307824 | tf_op jit(solution)/shard_map/convert_element_type | solution.py:117
  68.9 1.5 concatenate.22
  70.4 2.7 %reshape.328 = bf16[4,256,2,512]{3,2,1,0:T(2,128)(2,1)S(1)} reshape(bf16[4,512,512]{2,1,0:T(8,128)(2,1)} %concatenate.22) | data formatting | bytes 4194304 | tf_op jit(solution)/shard_map/reshape | solution.py:17
  73.2 3.0 %fusion.59 = (bf16[4,256,1,512]{3,2,1,0:T(2,128)(2,1)S(1)}, bf16[4,256,1,512]{3,2,1,0:T(2,128)(2,1)S(1)}) fusion(bf16[4,256,2,512]{3,2,1,0:T(2,128)(2,1)S(1)} %reshape.328), kind=kLoop, calls=%fused_computation.134 | loop fusion | bytes 4194304 | tf_op jit(solution)/shard_map/slice | solution.py:21
  76.7 1.3 fusion.60
  78.0 10.2 %fusion.27 = (bf16[4,255,512]{2,1,0:T(8,128)(2,1)S(1)}, bf16[4,255,512]{2,1,0:T(8,128)(2,1)}) fusion(bf16[4,255,512]{2,0,1:T(4,128)(2,1)} %param.15, f32[4,255]{1,0:T(4,128)S(1)} %fusion.47, bf16[512,1536]{1,0:T(8,128)(2,1)} %all-gather.5.cloned.1.call-done, bf16[4,255,512]{2,1,0:T(8,128)(2,1)} %get-tuple-element.41, bf16[4,255,512]{2,1,0:T(8,128)(2,1)S(1)} %bitcast.57, ...), kind=kOutput, calls=%fused_computation.53 | convolution fusion | flops 1654456320 | bytes 7843824 | tf_op jit(solution)/shard_map/dot_general | solution.py:120
  88.2 3.5 %convolution_bitcast_fusion.1 = f32[512,1536]{1,0:T(8,128)} fusion(bf16[4,255,512]{2,1,0:T(8,128)(2,1)S(1)} %get-tuple-element.36, bf16[4,255,512]{2,1,0:T(8,128)(2,1)S(1)} %copy-done.4, bf16[4,255,512]{2,1,0:T(8,128)(2,1)S(1)} %bitcast.58, bf16[4,255,512]{2,1,0:T(8,128)(2,1)S(1)} %get-tuple-element.40), kind=kOutput, calls=%fused_computation.40 | convolution fusion | flops 1613721600 | bytes 7323648 | tf_op jit(solution)/shard_map/dot_general | solution.py:140
  92.0 3.1 %copy.53 = bf16[4,255,512]{2,0,1:T(4,128)(2,1)} copy(bf16[4,255,512]{2,1,0:T(8,128)(2,1)} %get-tuple-element.37) | data formatting | bytes 2088960
  95.2 0.7 fusion.39
  95.9 0.7 fusion.40
  96.6 0.7 fusion.41
  97.3 2.2 pad_bitcast_fusion
  99.4 68.2 %reduce-scatter.2.cloned.1.call-done = f32[64,1536]{1,0:T(8,128)} async-done(((f32[512,1536]{1,0:T(8,128)}), f32[64,1536]{1,0:T(8,128)}) %reduce-scatter.2.cloned.1.call-update) | async-done | bytes 393232 | tf_op jit(solution)/shard_map/reduce_scatter | solution.py:139
  167.7 2.1 pad_maximum_fusion
  169.8 5.2 %copy.52 = f32[4,256,2,512]{3,2,1,0:T(2,128)} copy(f32[4,256,2,512]{3,1,0,2:T(8,128)S(1)} %pad_maximum_fusion) | data formatting | bytes 8388608 | tf_op jit(solution)/shard_map/stack | solution.py:38
  175.0 6.1 %reshape.329 = f32[4,512,512]{2,1,0:T(8,128)} reshape(f32[4,256,2,512]{3,2,1,0:T(2,128)} %copy.52) | data formatting | bytes 8388608 | tf_op jit(solution)/shard_map/reshape | solution.py:38
  181.1 6.0 %multiply_reduce_fusion.1 = (f32[4,512]{1,0:T(4,128)S(1)}, f32[512]{0:T(512)S(1)}, f32[4,512]{1,0:T(4,128)S(1)}, f32[512]{0:T(512)S(1)}, f32[4,511,512]{2,1,0:T(8,128)S(1)}) fusion(f32[4,511,512]{2,1,0:T(8,128)} %copy-done.1, f32[512]{0:T(512)S(1)} %copy-done.6, f32[4,512]{1,0:T(4,128)S(1)} %add_rsqrt_fusion, f32[4,512]{1,0:T(4,128)S(1)} %broadcast_divide_fusion.2, ...), kind=kLoop, calls=%fused_computation.15 | loop fusion | flops 21971968 | bytes 12607472 | tf_op jit(solution)/shard_map/reduce_sum | solution.py:154
  187.2 1.3 fusion.38
  188.5 39.9 %psum.7 = f32[512,12]{0,1:T(8,128)S(1)} all-reduce(f32[512,12]{0,1:T(8,128)S(1)} %pad_maximum_fusion.7), channel_id=1, replica_groups=mesh['dp'=8,'group'=4] {'dp','group'}, use_global_device_ids=true, to_apply=%region_11.12 | all-reduce | flops 6144 | bytes 49152 | tf_op jit(solution)/shard_map/psum | solution.py:165
  228.5 0.7 constant_dynamic-slice_fusion
  229.7 2.3 reduce_sum.95
  (58 shorter events, 4.0 us)
Async XLA Ops:
  7.2 11.1 %copy-start = (bf16[4,2560]{1,0:T(4,128)(2,1)S(1)}, bf16[4,2560]{1,0:T(4,128)(2,1)}, u32[]{:S(2)}) copy-start(bf16[4,2560]{1,0:T(4,128)(2,1)} %param.8) | copy-start | bytes 61444
  7.2 70.8 %all-gather.5.cloned.1.call-start = ((), (), s32[]{:S(2)}) async-start(), calls=%async_computation.2 | async-start | bytes 1769472 | tf_op jit(solution)/shard_map/all_gather | solution.py:119
  19.1 35.8 %all-to-all-start = ((bf16[4,2,2560]{2,1,0:T(2,128)(2,1)}), bf16[4,2,2560]{2,1,0:T(2,128)(2,1)S(1)}, u32[]{:S(2)}, u32[]{:S(2)}) async-start(bf16[4,2,2560]{2,1,0:T(2,128)(2,1)} %copy.42), calls=%async_computation | async-start | bytes 81920 | tf_op jit(solution)/shard_map/all_to_all | solution.py:81
  22.4 145.3 %reduce-scatter.2.cloned.1.call-start = ((), (), s32[]{:S(2)}) async-start(), calls=%async_computation.3 | async-start | bytes 3538944 | tf_op jit(solution)/shard_map/reduce_scatter | solution.py:139
  56.7 1.9 copy-start.5
  56.8 1.9 copy-start.6
  57.8 11.1 %copy-start.1 = (f32[4,511,512]{2,1,0:T(8,128)}, f32[4,511,512]{2,1,0:T(8,128)S(1)}, u32[]{:S(2)}) copy-start(f32[4,511,512]{2,1,0:T(8,128)S(1)} %get-tuple-element.51) | copy-start | bytes 12558340
  78.0 10.2 %copy-start.4 = (bf16[4,255,512]{2,1,0:T(8,128)(2,1)S(1)}, bf16[4,255,512]{2,1,0:T(8,128)(2,1)}, u32[]{:S(2)}) copy-start(bf16[4,255,512]{2,1,0:T(8,128)(2,1)} %get-tuple-element.41) | copy-start | bytes 3133444
  91.8 3.4 %copy-start.3 = (bf16[512,1536]{1,0:T(8,128)(2,1)S(1)}, bf16[512,1536]{1,0:T(8,128)(2,1)}, u32[]{:S(2)}) copy-start(bf16[512,1536]{1,0:T(8,128)(2,1)} %all-gather.5.cloned.1.call-done) | copy-start | bytes 4718596
  91.8 138.0 %all-gather.7.cloned.1.call-start = ((), (), s32[]{:S(2)}) async-start(), calls=%async_computation.4 | async-start | bytes 1966080 | tf_op jit(solution)/shard_map/all_gather | solution.py:147
  181.1 6.1 %copy-start.2 = (f32[4,511,512]{2,1,0:T(8,128)S(1)}, f32[4,511,512]{2,1,0:T(8,128)}, u32[]{:S(2)}) copy-start(f32[4,511,512]{2,1,0:T(8,128)} %copy-done.1) | copy-start | bytes 12558340
Sparse Core Ops, SparseCore 0:
  10.2 47.2 all-gather.4
  91.9 75.7 reduce-scatter.1
  169.2 18.7 all-gather.6
